TPU v7x, 128 devices: a whole 4x4x4 slice. The times are simulated.
128 devices in a mesh: pair: 32 (over z, y, x_lo), chol: 4 (over x_hi, core).
Axes of the slice: x: 4 (x_hi: 2, x_lo: 2; x = x_hi * 2 + x_lo), y: 4, z: 4, core: 2. Of those that a mesh axis runs over, the one named last changes fastest.
Arguments:
- left_vectors: bfloat16 [8, 160, 800], P(None, 'pair'), may hold values from -6 to 6
- chol_factors: bfloat16 [160, 800, 2560], P('pair', None, 'chol'), may hold values from -0.046875 to 0.046875
- eps_occ: float32 [160], P('pair'), may hold values from -1.5 to -0.3
- eps_vir: float32 [800], replicated, may hold values from 0.2 to 3
Outputs:
- left_sigma: float32 [8, 160, 800], P(None, 'pair')
All inputs are finite; a program needn't handle non-finite values.
Results may differ from a plain program's by a relative error of at most 0.0016.
Values may be sent and summed in bfloat16 or wider, within the bound.
No kernel may reach another device: no remote copies, remote signals or barrier semaphores. Data moves between devices by JAX's collectives and lax.ppermute only.
A program may use at most 64 MiB of HBM per device.

v0:
```python
import jax
import jax.numpy as jnp
from jax import lax
from jax.sharding import PartitionSpec as P


def body(left_vectors, chol_factors, eps_occ, eps_vir):
    occ_local = chol_factors.shape[0]
    gathered = lax.all_gather(left_vectors, "pair", axis=1, tiled=True)
    coul_part = jnp.einsum(
        "ria,iap->rp", left_vectors, chol_factors, preferred_element_type=jnp.float32
    )
    coul_vec = lax.psum(coul_part, "pair").astype(jnp.bfloat16)
    coulomb = jnp.einsum("iap,rp->ria", chol_factors, coul_vec, preferred_element_type=jnp.float32)
    z_local = jnp.einsum(
        "ibp,rjb->rijp", chol_factors, gathered, preferred_element_type=jnp.float32
    ).astype(jnp.bfloat16)
    exchange_term = jnp.einsum(
        "rijp,jap->ria",
        lax.all_to_all(z_local, "pair", split_axis=2, concat_axis=1, tiled=True),
        chol_factors,
        preferred_element_type=jnp.float32,
    )
    offset = lax.axis_index("pair") * occ_local
    partial_all = -exchange_term
    own_rows = lax.dynamic_slice_in_dim(partial_all, offset, occ_local, 1) + 2.0 * coulomb
    partial_all = lax.dynamic_update_slice_in_dim(partial_all, own_rows, offset, 1)
    summed_all = lax.psum(partial_all, ("pair", "chol"))
    summed = lax.dynamic_slice_in_dim(summed_all, offset, occ_local, 1)
    diagonal_part = (eps_vir[None, None, :] - eps_occ[None, :, None]) * left_vectors.astype(
        jnp.float32
    )
    return diagonal_part + summed


def solution(mesh):
    placed = (P(None, "pair", None), P("pair", None, "chol"), P("pair"), P())
    return jax.shard_map(
        body, mesh=mesh, in_specs=placed, out_specs=P(None, "pair", None), check_vma=False
    )
```

profile of v0, /device:TPU:1, one launch (start us, length us, event | category | flops | bytes accessed | tf_op | source)
XLA Modules:
  0.0 612.2 jit_solution(9357112869376586982)
XLA Ops:
  6.5 0.0 all-gather.2.cloned.1.call-start
  6.5 0.7 all-gather.2.cloned.1.call-update
  7.3 140.7 %all-gather.2.cloned.1.call-done = bf16[8,160,800]{2,0,1:T(8,128)(2,1)} async-done(((bf16[8,5,800]{2,0,1:T(8,128)(2,1)}), bf16[8,160,800]{2,0,1:T(8,128)(2,1)}) %all-gather.2.cloned.1.call-update) | async-done | bytes 2048016 | tf_op jit(solution)/shard_map/all_gather | solution.py:9
  147.9 11.9 %convert_bitcast_fusion = bf16[8,5,160,640]{3,2,1,0:T(8,128)(2,1)S(1)} fusion(bf16[5,800,640]{2,1,0:T(8,128)(2,1)} %param.5, bf16[8,160,800,1]{2,0,1,3:T(8,128)(2,1)} %bitcast.28), kind=kOutput, calls=%fused_computation | convolution fusion | flops 6557696000 | bytes 15360000 | tf_op jit(solution)/shard_map/ibp,rjb->rijp/dot_general | solution.py:15
  159.9 6.1 copy.34
  166.0 7.0 %all-to-all-start = ((bf16[8,5,160,640]{3,0,1,2:T(8,128)(2,1)}), bf16[8,5,160,640]{3,0,1,2:T(8,128)(2,1)}, u32[]{:S(2)}, u32[]{:S(2)}) async-start(bf16[8,5,160,640]{3,0,1,2:T(8,128)(2,1)} %copy.34), calls=%async_computation | async-start | bytes 16384000 | tf_op jit(solution)/shard_map/all_to_all | solution.py:20
  173.0 0.0 all-reduce.2.cloned.1.call-start
  173.0 0.0 copy-done
  173.0 0.0 slice-start
  173.1 3.3 convolution_bitcast_fusion
  176.4 206.2 %psum.14 = bf16[8,640]{1,0:T(8,128)(2,1)S(1)} all-reduce(f32[8,640]{1,0:T(8,128)S(1)} %convolution_bitcast_fusion), channel_id=1, replica_groups=mesh['pair'=32,'chol'=4] {'pair'}, use_global_device_ids=true, to_apply=%region_0.0 | all-reduce | flops 5120 | bytes 30720 | tf_op jit(solution)/shard_map/psum | solution.py:13
  382.6 0.0 all-to-all-done
  382.6 0.0 slice-start.1
  382.6 7.3 %copy.36 = bf16[8,32,5,5,640]{4,0,3,2,1:T(8,128)(2,1)} copy(bf16[8,32,5,5,640]{4,0,2,3,1:T(8,128)(2,1)} %bitcast.5) | data formatting | bytes 16384000 | tf_op jit(solution)/shard_map/all_to_all | solution.py:20
  389.9 0.0 slice-done
  390.0 0.0 slice-done.1
  390.0 12.7 %bitcast_negate_fusion = f32[8,160,800]{2,0,1:T(8,128)} fusion(bf16[8,160,5,640]{3,0,2,1:T(8,128)(2,1)} %bitcast.27, bf16[5,800,640]{2,1,0:T(8,128)(2,1)S(1)} %bitcast.26), kind=kOutput, calls=%fused_computation.4 | convolution fusion | flops 6554624000 | bytes 17408000 | tf_op jit(solution)/shard_map/rijp,jap->ria/dot_general | solution.py:18
  402.6 3.1 fusion.7
  405.7 0.0 all-reduce.2.cloned.1.call-update
  405.7 0.0 copy-done.1
  405.8 0.0 copy-done.2
  405.8 0.1 broadcast_subtract_fusion
  405.8 198.0 %all-reduce.2.cloned.1.call-done = f32[8,160,800]{2,0,1:T(8,128)} async-done(((f32[8,160,800]{2,0,1:T(8,128)}), f32[8,160,800]{2,0,1:T(8,128)}) %all-reduce.2.cloned.1.call-update) | async-done | bytes 4096016 | tf_op jit(solution)/shard_map/psum | solution.py:28
  603.8 1.6 dynamic-slice_add_fusion
  (4 shorter events, 0.0 us)
Async XLA Ops:
  6.5 141.4 %all-gather.2.cloned.1.call-start = ((), (), s32[]{:S(2)}) async-start(), calls=%async_computation.1 | async-start | bytes 2365440 | tf_op jit(solution)/shard_map/all_gather | solution.py:9
  166.0 7.1 %copy-start = (bf16[8,5,800]{2,0,1:T(8,128)(2,1)S(1)}, bf16[8,5,800]{2,0,1:T(8,128)(2,1)}, u32[]{:S(2)}) copy-start(bf16[8,5,800]{2,0,1:T(8,128)(2,1)} %param.4) | copy-start | bytes 192004
  166.0 216.6 %all-to-all-start = ((bf16[8,5,160,640]{3,0,1,2:T(8,128)(2,1)}), bf16[8,5,160,640]{3,0,1,2:T(8,128)(2,1)}, u32[]{:S(2)}, u32[]{:S(2)}) async-start(bf16[8,5,160,640]{3,0,1,2:T(8,128)(2,1)} %copy.34), calls=%async_computation | async-start | bytes 16384000 | tf_op jit(solution)/shard_map/all_to_all | solution.py:20
  173.0 430.8 %all-reduce.2.cloned.1.call-start = ((), (), s32[]{:S(2)}) async-start(), calls=%async_computation.2 | async-start | bytes 9175040 | tf_op jit(solution)/shard_map/psum | solution.py:28
  173.0 216.9 %slice-start = ((s8[5120000]{0:T(1024)(128)(4,1)}), s8[925696]{0:T(1024)(128)(4,1)S(1)}, s32[]{:S(2)}) async-start(s8[5120000]{0:T(1024)(128)(4,1)} %bitcast.25), calls=%async_computation.3 | async-start | bytes 1851392
  382.6 7.3 %slice-start.1 = ((s8[5120000]{0:T(1024)(128)(4,1)}), s8[4194304]{0:T(1024)(128)(4,1)S(1)}, s32[]{:S(2)}) async-start(s8[5120000]{0:T(1024)(128)(4,1)} %bitcast.25), calls=%async_computation.4 | async-start | bytes 8388608
  402.6 3.1 copy-start.1
  402.6 3.1 copy-start.2
Sparse Core Ops, SparseCore 0:
  9.0 138.8 all-gather.1
  405.9 197.8 all-reduce.1
where the time goes:
time: 612 us
  waiting for transfers between devices  339 us (55%)
  blocking collectives  206 us (34%)
  matrix products  31 us (5%)
  local copies, waits for them, and re-layouts  13.5 us (2%)
  between operations  13.5 us (2%)
  starting transfers between devices  7.04 us (1%)
    psum x1, blocking collectives, body(): coul_vec = lax.psum(coul_part, 'pair').astype(jnp.bfloat16)  206 us
    psum x1, waiting for transfers between devices, body(): summed_all = lax.psum(partial_all, ('pair', 'chol'))  198 us
    all_gather x1, waiting for transfers between devices, body(): gathered = lax.all_gather(left_vectors, 'pair', axis=1, tiled=True)  141 us
    dot_general x1, matrix products, body(): jnp.einsum('rijp,jap->ria', lax.all_to_all(z_local, 'pair', split_axis=2,...  12.7 us
  transfers between devices with their start and end apart: 3, of which 2 were waited for; matrix products, arithmetic and copies ran while one was open for 1% of the time, Pallas kernels for 0%

commit v1 on v0

--- a/solution.py
+++ b/solution.py
@@ -25,7 +25,7 @@
     partial_all = -exchange_term
     own_rows = lax.dynamic_slice_in_dim(partial_all, offset, occ_local, 1) + 2.0 * coulomb
     partial_all = lax.dynamic_update_slice_in_dim(partial_all, own_rows, offset, 1)
-    summed_all = lax.psum(partial_all, ("pair", "chol"))
+    summed_all = lax.psum(lax.psum(partial_all, "chol"), "pair")
     summed = lax.dynamic_slice_in_dim(summed_all, offset, occ_local, 1)
     diagonal_part = (eps_vir[None, None, :] - eps_occ[None, :, None]) * left_vectors.astype(
         jnp.float32

time: 612 us -> 896 us (1.46)
  the two profiles are of different devices: /device:TPU:1 before, /device:TPU:0 now
where the time goes in v1:
time: 896 us
  waiting for transfers between devices  597 us (67%)
  blocking collectives  232 us (26%)
  matrix products  31 us (3%)
  local copies, waits for them, and re-layouts  13.5 us (2%)
  between operations  13.2 us (1%)
    psum x2, waiting for transfers between devices, body(): summed_all = lax.psum(lax.psum(partial_all, 'chol'), 'pair')  436 us
    psum x1, blocking collectives, body(): coul_vec = lax.psum(coul_part, 'pair').astype(jnp.bfloat16)  232 us
    all_gather x1, waiting for transfers between devices, body(): gathered = lax.all_gather(left_vectors, 'pair', axis=1, tiled=True)  160 us
  transfers between devices with their start and end apart: 4, of which 3 were waited for; matrix products, arithmetic and copies ran while one was open for 0% of the time, Pallas kernels for 0%

profile of v1, /device:TPU:0, one launch (start us, length us, event | category | flops | bytes accessed | tf_op | source)
XLA Modules:
  0.0 895.5 jit_solution(1680119577524978352)
XLA Ops:
  6.5 0.0 all-gather.2.cloned.1.call-start
  6.5 0.7 all-gather.2.cloned.1.call-update
  7.3 160.4 %all-gather.2.cloned.1.call-done = bf16[8,160,800]{2,0,1:T(8,128)(2,1)} async-done(((bf16[8,5,800]{2,0,1:T(8,128)(2,1)}), bf16[8,160,800]{2,0,1:T(8,128)(2,1)}) %all-gather.2.cloned.1.call-update) | async-done | bytes 2048016 | tf_op jit(solution)/shard_map/all_gather | solution.py:9
  167.6 11.9 %convert_bitcast_fusion = bf16[8,5,160,640]{3,2,1,0:T(8,128)(2,1)S(1)} fusion(bf16[5,800,640]{2,1,0:T(8,128)(2,1)} %param.5, bf16[8,160,800,1]{2,0,1,3:T(8,128)(2,1)} %bitcast.28), kind=kOutput, calls=%fused_computation | convolution fusion | flops 6557696000 | bytes 15360000 | tf_op jit(solution)/shard_map/ibp,rjb->rijp/dot_general | solution.py:15
  179.6 6.1 copy.34
  185.7 7.6 all-to-all-start
  193.3 0.0 all-reduce.3.cloned.1.call-start
  193.3 0.0 copy-done
  193.4 0.0 slice-start
  193.4 3.3 convolution_bitcast_fusion
  196.7 231.7 %psum.21 = bf16[8,640]{1,0:T(8,128)(2,1)S(1)} all-reduce(f32[8,640]{1,0:T(8,128)S(1)} %convolution_bitcast_fusion), channel_id=1, replica_groups=mesh['pair'=32,'chol'=4] {'pair'}, use_global_device_ids=true, to_apply=%region_0.0 | all-reduce | flops 5120 | bytes 30720 | tf_op jit(solution)/shard_map/psum | solution.py:13
  428.4 0.0 all-to-all-done
  428.4 7.3 copy.36
  435.7 0.0 slice-done
  435.7 0.0 slice-done.1
  435.7 12.7 %bitcast_negate_fusion = f32[8,160,800]{2,0,1:T(8,128)} fusion(bf16[8,160,5,640]{3,0,2,1:T(8,128)(2,1)} %bitcast.27, bf16[5,800,640]{2,1,0:T(8,128)(2,1)S(1)} %bitcast.26), kind=kOutput, calls=%fused_computation.4 | convolution fusion | flops 6554624000 | bytes 17408000 | tf_op jit(solution)/shard_map/rijp,jap->ria/dot_general | solution.py:18
  448.5 3.1 fusion.7
  451.5 0.0 all-reduce.3.cloned.1.call-update
  451.6 0.0 all-reduce.5.cloned.1.call-start
  451.6 94.9 %all-reduce.3.cloned.1.call-done = f32[8,160,800]{2,0,1:T(8,128)} async-done(((f32[8,160,800]{2,0,1:T(8,128)}), f32[8,160,800]{2,0,1:T(8,128)}) %all-reduce.3.cloned.1.call-update) | async-done | bytes 4096016 | tf_op jit(solution)/shard_map/psum | solution.py:28
  546.5 0.0 all-reduce.5.cloned.1.call-update
  546.6 0.1 broadcast_subtract_fusion
  546.6 340.8 %all-reduce.5.cloned.1.call-done = f32[8,160,800]{2,0,1:T(8,128)} async-done(((f32[8,160,800]{2,0,1:T(8,128)}), f32[8,160,800]{2,0,1:T(8,128)}) %all-reduce.5.cloned.1.call-update) | async-done | bytes 4096016 | tf_op jit(solution)/shard_map/psum | solution.py:28
  887.4 1.6 dynamic-slice_add_fusion
  (7 shorter events, 0.0 us)
Async XLA Ops:
  6.5 161.1 %all-gather.2.cloned.1.call-start = ((), (), s32[]{:S(2)}) async-start(), calls=%async_computation.1 | async-start | bytes 2365440 | tf_op jit(solution)/shard_map/all_gather | solution.py:9
  185.7 7.6 copy-start
  185.7 242.7 %all-to-all-start = ((bf16[8,5,160,640]{3,0,1,2:T(8,128)(2,1)}), bf16[8,5,160,640]{3,0,1,2:T(8,128)(2,1)}, u32[]{:S(2)}, u32[]{:S(2)}) async-start(bf16[8,5,160,640]{3,0,1,2:T(8,128)(2,1)} %copy.34), calls=%async_computation | async-start | bytes 16384000 | tf_op jit(solution)/shard_map/all_to_all | solution.py:20
  193.3 353.2 %all-reduce.3.cloned.1.call-start = ((), (), s32[]{:S(2)}) async-start(), calls=%async_computation.2 | async-start | bytes 9175040 | tf_op jit(solution)/shard_map/psum | solution.py:28
  193.4 242.4 %slice-start = ((s8[5120000]{0:T(1024)(128)(4,1)}), s8[925696]{0:T(1024)(128)(4,1)S(1)}, s32[]{:S(2)}) async-start(s8[5120000]{0:T(1024)(128)(4,1)} %bitcast.25), calls=%async_computation.4 | async-start | bytes 1851392
  428.4 7.3 slice-start.1
  451.5 95.0 %copy-start.1 = (f32[800]{0:T(1024)S(1)}, f32[800]{0:T(1024)}, u32[]{:S(2)}) copy-start(f32[800]{0:T(1024)} %param.7) | copy-start | bytes 9604
  451.5 95.0 %copy-start.2 = (f32[5]{0:T(128)S(1)}, f32[5]{0:T(128)}, u32[]{:S(2)}) copy-start(f32[5]{0:T(128)} %param.6) | copy-start | bytes 64
  451.6 435.9 %all-reduce.5.cloned.1.call-start = ((), (), s32[]{:S(2)}) async-start(), calls=%async_computation.3 | async-start | bytes 9175040 | tf_op jit(solution)/shard_map/psum | solution.py:28
Sparse Core Ops, SparseCore 0:
  9.0 158.6 all-gather.1
  451.7 94.8 all-reduce.2
  549.1 338.3 all-reduce.4
